TPU v7x, 256 devices: a whole 4x4x8 slice. The times are simulated.
256 devices in a mesh: seq: 16 (over z, core), head: 8 (over x_lo, y), batch: 2 (over x_hi).
Axes of the slice: x: 4 (x_hi: 2, x_lo: 2; x = x_hi * 2 + x_lo), y: 4, z: 8, core: 2. Of those that a mesh axis runs over, the one named last changes fastest.
Arguments:
- queries: bfloat16 [8192, 4096], P(('batch', 'seq'), 'head'), parts along dimension 0, may hold values from -16 to 16, as said below
- key_rows: bfloat16 [8192, 1024], P(('batch', 'seq'), 'head'), parts along dimension 0, may hold values from -16 to 16
- value_rows: bfloat16 [8192, 1024], P(('batch', 'seq'), 'head'), parts along dimension 0, may hold values from -6 to 6
- out_grad: bfloat16 [8192, 4096], P(('batch', 'seq'), 'head'), parts along dimension 0, may hold values from -6 to 6
- tile_ids: int32 [64], P('batch'), parts along dimension 0, may hold values from 0 to 31, each once
- tile_mask: int32 [64, 32], P('batch'), parts along dimension 0, may hold values from 0 to 1, as said below
Outputs:
- attended: bfloat16 [8192, 4096], P(('batch', 'seq'), 'head'), parts along dimension 0
- query_grad: float32 [8192, 4096], P(('batch', 'seq'), 'head'), parts along dimension 0
- key_grad: float32 [8192, 1024], P(('batch', 'seq'), 'head'), parts along dimension 0
- value_grad: float32 [8192, 1024], P(('batch', 'seq'), 'head'), parts along dimension 0
There are 2 independent parts, one for each index of `batch`. A program takes and returns all parts, laid end to end along the dimension named above; each array names one. Nothing has to cross between parts.
Inputs may be any that keep to these rules, and one draw needn't show every extreme that they name: `queries`: in the hidden draw a few query rows equal scaled key rows of the same tile. `tile_mask`: 1 only where the key tile's index is at most the query tile's; 1 on the diagonal.
All inputs are finite; a program needn't handle non-finite values.
Results may differ from a plain program's by a relative error of at most 0.03.
Values may be sent and summed in bfloat16 or wider, within the bound.
A program may use at most 64 MiB of HBM per device.

v0:
```python
import math
import jax
import jax.numpy as jnp
from jax import lax
from jax.sharding import PartitionSpec as P

HD = 128
TILE = 128
far_below = -1e30


def tile_allowed(tile_mask, query_tiles, key_tiles):
    table = jnp.take(jnp.take(tile_mask, query_tiles, axis=0), key_tiles, axis=1) == 1
    same_tile = query_tiles[:, None] == key_tiles[None, :]
    inside = lax.broadcasted_iota(jnp.int32, (TILE, TILE), 0) >= lax.broadcasted_iota(
        jnp.int32, (TILE, TILE), 1
    )
    full = table[:, None, :, None] & (
        jnp.logical_not(same_tile)[:, None, :, None] | inside[None, :, None, :]
    )
    return full.reshape(query_tiles.shape[0] * TILE, key_tiles.shape[0] * TILE)


def sub_blocks(row_total, limit):
    block_rows = math.gcd(row_total, limit)
    return (block_rows, row_total // block_rows)


def per_device(queries, key_rows, value_rows, out_grad, tile_ids, tile_mask):
    row_count = queries.shape[0]
    group_count = key_rows.shape[1] // HD
    head_count = queries.shape[1] // (group_count * HD)
    factor = HD ** (-0.5)
    my_rank = lax.axis_index("seq")
    limit = 1024
    query_heads = queries.reshape(row_count, group_count, head_count, HD)
    grad_heads = out_grad.reshape(row_count, group_count, head_count, HD)
    query_tiles = lax.dynamic_slice_in_dim(
        tile_ids, my_rank * (row_count // TILE), row_count // TILE
    )

    def block_mask(first_row, row_total):
        key_tiles = lax.dynamic_slice_in_dim(tile_ids, first_row // TILE, row_total // TILE)
        return tile_allowed(tile_mask, query_tiles, key_tiles)

    def masked_scores(key_block, allowed):
        scores = (
            jnp.einsum("qghd,kgd->ghqk", query_heads, key_block, preferred_element_type=jnp.float32)
            * factor
        )
        return jnp.where(allowed[None, None], scores, far_below)

    def forward_block(carried, key_block, value_block, first_row):
        allowed = block_mask(first_row, key_block.shape[0])
        row_max, denominator, weighted = carried
        scores = masked_scores(key_block, allowed)
        new_max = jnp.maximum(row_max, jnp.max(scores, axis=-1))
        shrink = jnp.exp(row_max - new_max)
        softmax_terms = jnp.where(allowed[None, None], jnp.exp(scores - new_max[..., None]), 0.0)
        denominator = denominator * shrink + jnp.sum(softmax_terms, axis=-1)
        weighted = weighted * shrink[..., None] + jnp.einsum(
            "ghqk,kgd->ghqd",
            softmax_terms.astype(jnp.bfloat16),
            value_block,
            preferred_element_type=jnp.float32,
        )
        return (new_max, denominator, weighted)

    stat_shape = (group_count, head_count, row_count)
    initial = (
        jnp.full(stat_shape, far_below, jnp.float32),
        jnp.zeros(stat_shape, jnp.float32),
        jnp.zeros(stat_shape + (HD,), jnp.float32),
    )
    key_piece = lax.all_gather(key_rows, "seq", axis=0, tiled=True)
    value_piece = lax.all_gather(value_rows, "seq", axis=0, tiled=True)
    block_rows, number = sub_blocks(key_piece.shape[0], limit)

    def forward_advance(position, current):
        key_block = lax.dynamic_slice_in_dim(key_piece, position * block_rows, block_rows).reshape(
            block_rows, group_count, HD
        )
        value_block = lax.dynamic_slice_in_dim(
            value_piece, position * block_rows, block_rows
        ).reshape(block_rows, group_count, HD)
        return forward_block(current, key_block, value_block, position * block_rows)

    row_max, denominator, weighted = lax.fori_loop(0, number, forward_advance, initial)
    attended_heads = jnp.transpose(weighted / denominator[..., None], (2, 0, 1, 3))
    attended = attended_heads.reshape(row_count, group_count * head_count * HD).astype(jnp.bfloat16)
    log_total = row_max + jnp.log(denominator)
    row_delta = jnp.transpose(
        jnp.sum(
            grad_heads.astype(jnp.float32)
            * attended.reshape(row_count, group_count, head_count, HD).astype(jnp.float32),
            axis=-1,
        ),
        (1, 2, 0),
    )

    def backward_block(key_block, value_block, first_row):
        allowed = block_mask(first_row, key_block.shape[0])
        scores = masked_scores(key_block, allowed)
        softmax_terms = jnp.where(allowed[None, None], jnp.exp(scores - log_total[..., None]), 0.0)
        dprobs = jnp.einsum(
            "qghd,kgd->ghqk", grad_heads, value_block, preferred_element_type=jnp.float32
        )
        dscores = (softmax_terms * (dprobs - row_delta[..., None])).astype(jnp.bfloat16)
        query_part = (
            jnp.einsum("ghqk,kgd->qghd", dscores, key_block, preferred_element_type=jnp.float32)
            * factor
        )
        key_part = (
            jnp.einsum("ghqk,qghd->kgd", dscores, query_heads, preferred_element_type=jnp.float32)
            * factor
        )
        value_part = jnp.einsum(
            "ghqk,qghd->kgd",
            softmax_terms.astype(jnp.bfloat16),
            grad_heads,
            preferred_element_type=jnp.float32,
        )
        key_flat = key_part.reshape(key_block.shape[0], group_count * HD)
        value_flat = value_part.reshape(key_block.shape[0], group_count * HD)
        return (query_part, jnp.concatenate([key_flat, value_flat], axis=-1))

    gathered_keys, gathered_values = (
        lax.all_gather(key_rows, "seq", axis=0, tiled=True),
        lax.all_gather(value_rows, "seq", axis=0, tiled=True),
    )
    sweep_block_rows, number = sub_blocks(gathered_keys.shape[0], limit)

    def sweep_advance(query_sum, position):
        key_block = lax.dynamic_slice_in_dim(
            gathered_keys, position * sweep_block_rows, sweep_block_rows
        ).reshape(sweep_block_rows, group_count, HD)
        value_block = lax.dynamic_slice_in_dim(
            gathered_values, position * sweep_block_rows, sweep_block_rows
        ).reshape(sweep_block_rows, group_count, HD)
        query_part, key_value = backward_block(
            key_block, value_block, 0 + position * sweep_block_rows
        )
        return (query_sum + query_part, key_value)

    query_sum, stacked = lax.scan(
        sweep_advance,
        jnp.zeros((row_count, group_count, head_count, HD), jnp.float32),
        jnp.arange(number, dtype=jnp.int32),
    )
    query_sum, key_terms = (
        query_sum,
        stacked.reshape(gathered_keys.shape[0], 2 * group_count * HD),
    )
    own_terms = lax.psum_scatter(
        key_terms.astype(jnp.bfloat16), "seq", scatter_dimension=0, tiled=True
    ).astype(jnp.float32)
    query_grad = query_sum.reshape(row_count, group_count * head_count * HD)
    width = group_count * HD
    return (attended, query_grad, own_terms[:, :width], own_terms[:, width:])


def solution(mesh):
    return jax.shard_map(
        per_device,
        mesh=mesh,
        in_specs=(
            P(("batch", "seq"), "head"),
            P(("batch", "seq"), "head"),
            P(("batch", "seq"), "head"),
            P(("batch", "seq"), "head"),
            P("batch"),
            P("batch", None),
        ),
        out_specs=(
            P(("batch", "seq"), "head"),
            P(("batch", "seq"), "head"),
            P(("batch", "seq"), "head"),
            P(("batch", "seq"), "head"),
        ),
        check_vma=False,
    )
```

profile of v0, /device:TPU:2, one launch (start us, length us, event | category | flops | bytes accessed | tf_op | source)
XLA Modules:
  0.0 242.3 jit_solution(15315642816570585273)
XLA Ops:
  12.6 38.7 %all-gather.3.cloned.1.call-done = bf16[4096,128]{1,0:T(8,128)(2,1)} async-done(((bf16[256,128]{1,0:T(8,128)(2,1)}), bf16[4096,128]{1,0:T(8,128)(2,1)}) %all-gather.3.cloned.1.call-update) | async-done | bytes 1048592 | tf_op jit(solution)/shard_map/all_gather | solution.py:75
  51.4 39.0 %all-gather.5.cloned.1.call-done = bf16[4096,128]{1,0:T(8,128)(2,1)} async-done(((bf16[256,128]{1,0:T(8,128)(2,1)}), bf16[4096,128]{1,0:T(8,128)(2,1)}) %all-gather.5.cloned.1.call-update) | async-done | bytes 1048592 | tf_op jit(solution)/shard_map/all_gather | solution.py:76
  90.3 30.9 %while.35 = (s32[]{:T(128)}, f32[1,4,256]{2,1,0:T(4,128)S(1)}, f32[1,4,256]{2,1,0:T(4,128)S(1)}, f32[1,4,256,128]{3,2,1,0:T(8,128)S(1)}, s32[32]{0:T(128)}, /*in...) while((s32[]{:T(128)}, f32[1,4,256]{2,1,0:T(4,128)S(1)}, ...), condition=%wide.region_3.6_spmd.clone, body=%wide.region_0.5_spmd.clone.sunk | while | flops 551443584 | bytes 16618426 | solution.py:88
  92.7 1.8 fusion.100
  95.5 2.4 %fusion.103 = f32[1,4,256,128]{3,2,1,0:T(8,128)S(1)} fusion(f32[1024,256,4]{1,0,2:T(8,128)S(1)} %get-tuple-element.745, f32[4,256]{1,0:T(4,128)S(1)} %bitcast.245, pred[256,1024]{0,1:T(8,128)(4,1)S(1)} %copy.70, f32[1,4,256,128]{3,2,1,0:T(8,128)S(1)} %get-tuple-element.783, bf16[4096,128]{1,0:T(8,128)(2,1)} %get-tuple-element.807, ...), kind=kOutput, calls=%fused_computation.12.clone.1 | convolution fusion | flops 274071552 | bytes 5775365 | tf_op jit(solution)/shard_map/while/body/eval_jaxpr/ghqk,kgd->ghqd/dot_general | solution.py:61
  100.4 1.8 fusion.100
  103.3 2.4 %fusion.103 = f32[1,4,256,128]{3,2,1,0:T(8,128)S(1)} fusion(f32[1024,256,4]{1,0,2:T(8,128)S(1)} %get-tuple-element.745, f32[4,256]{1,0:T(4,128)S(1)} %bitcast.245, pred[256,1024]{0,1:T(8,128)(4,1)S(1)} %copy.70, f32[1,4,256,128]{3,2,1,0:T(8,128)S(1)} %get-tuple-element.783, bf16[4096,128]{1,0:T(8,128)(2,1)} %get-tuple-element.807, ...), kind=kOutput, calls=%fused_computation.12.clone.1 | convolution fusion | flops 274071552 | bytes 5775365 | tf_op jit(solution)/shard_map/while/body/eval_jaxpr/ghqk,kgd->ghqd/dot_general | solution.py:61
  108.2 1.8 fusion.100
  111.0 2.4 %fusion.103 = f32[1,4,256,128]{3,2,1,0:T(8,128)S(1)} fusion(f32[1024,256,4]{1,0,2:T(8,128)S(1)} %get-tuple-element.745, f32[4,256]{1,0:T(4,128)S(1)} %bitcast.245, pred[256,1024]{0,1:T(8,128)(4,1)S(1)} %copy.70, f32[1,4,256,128]{3,2,1,0:T(8,128)S(1)} %get-tuple-element.783, bf16[4096,128]{1,0:T(8,128)(2,1)} %get-tuple-element.807, ...), kind=kOutput, calls=%fused_computation.12.clone.1 | convolution fusion | flops 274071552 | bytes 5775365 | tf_op jit(solution)/shard_map/while/body/eval_jaxpr/ghqk,kgd->ghqd/dot_general | solution.py:61
  115.9 1.8 fusion.100
  118.8 2.4 %fusion.103 = f32[1,4,256,128]{3,2,1,0:T(8,128)S(1)} fusion(f32[1024,256,4]{1,0,2:T(8,128)S(1)} %get-tuple-element.745, f32[4,256]{1,0:T(4,128)S(1)} %bitcast.245, pred[256,1024]{0,1:T(8,128)(4,1)S(1)} %copy.70, f32[1,4,256,128]{3,2,1,0:T(8,128)S(1)} %get-tuple-element.783, bf16[4096,128]{1,0:T(8,128)(2,1)} %get-tuple-element.807, ...), kind=kOutput, calls=%fused_computation.12.clone.1 | convolution fusion | flops 274071552 | bytes 5775365 | tf_op jit(solution)/shard_map/while/body/eval_jaxpr/ghqk,kgd->ghqd/dot_general | solution.py:61
  121.6 49.8 %while.36 = (s32[]{:T(128)}, f32[256,1,4,128]{0,3,2,1:T(8,128)S(1)}, bf16[4,1024,256]{1,2,0:T(8,128)(2,1)}, s32[4]{0:T(128)S(1)}, bf16[4096,128]{1,0:T(8,128)(2,...) while((s32[]{:T(128)}, ...), condition=%wide.region_6.9_spmd.clone, body=%wide.region_5.8_spmd.clone.sunk | while | flops 1357005952 | bytes 25215972 | solution.py:145
  125.3 1.6 fusion.114
  126.9 1.5 fusion.117
  128.4 2.5 %fusion.115 = bf16[1,4,256,1024]{2,3,1,0:T(8,128)(2,1)S(1)} fusion(f32[1024,256,4]{1,0,2:T(8,128)S(1)} %fusion.114, f32[4,256]{1,0:T(4,128)S(1)} %bitcast.251, f32[4,256]{1,0:T(4,128)S(1)} %bitcast.253, pred[256,1024]{0,1:T(8,128)(4,1)S(1)} %copy.73, bf16[256,1,4,128]{0,3,2,1:T(8,128)(2,1)S(1)} %get-tuple-element.869, ...), kind=kOutput, calls=%fused_computation.40.clone.1 | convolution fusion | flops 275775488 | bytes 7086084 | tf_op jit(solution)/shard_map/while/body/eval_jaxpr/qghd,kgd->ghqk/dot_general | solution.py:105
  137.7 1.6 fusion.114
  140.9 2.5 %fusion.115 = bf16[1,4,256,1024]{2,3,1,0:T(8,128)(2,1)S(1)} fusion(f32[1024,256,4]{1,0,2:T(8,128)S(1)} %fusion.114, f32[4,256]{1,0:T(4,128)S(1)} %bitcast.251, f32[4,256]{1,0:T(4,128)S(1)} %bitcast.253, pred[256,1024]{0,1:T(8,128)(4,1)S(1)} %copy.73, bf16[256,1,4,128]{0,3,2,1:T(8,128)(2,1)S(1)} %get-tuple-element.869, ...), kind=kOutput, calls=%fused_computation.40.clone.1 | convolution fusion | flops 275775488 | bytes 7086084 | tf_op jit(solution)/shard_map/while/body/eval_jaxpr/qghd,kgd->ghqk/dot_general | solution.py:105
  150.2 1.6 fusion.114
  153.4 2.5 %fusion.115 = bf16[1,4,256,1024]{2,3,1,0:T(8,128)(2,1)S(1)} fusion(f32[1024,256,4]{1,0,2:T(8,128)S(1)} %fusion.114, f32[4,256]{1,0:T(4,128)S(1)} %bitcast.251, f32[4,256]{1,0:T(4,128)S(1)} %bitcast.253, pred[256,1024]{0,1:T(8,128)(4,1)S(1)} %copy.73, bf16[256,1,4,128]{0,3,2,1:T(8,128)(2,1)S(1)} %get-tuple-element.869, ...), kind=kOutput, calls=%fused_computation.40.clone.1 | convolution fusion | flops 275775488 | bytes 7086084 | tf_op jit(solution)/shard_map/while/body/eval_jaxpr/qghd,kgd->ghqk/dot_general | solution.py:105
  162.6 1.6 fusion.114
  165.8 2.5 %fusion.115 = bf16[1,4,256,1024]{2,3,1,0:T(8,128)(2,1)S(1)} fusion(f32[1024,256,4]{1,0,2:T(8,128)S(1)} %fusion.114, f32[4,256]{1,0:T(4,128)S(1)} %bitcast.251, f32[4,256]{1,0:T(4,128)S(1)} %bitcast.253, pred[256,1024]{0,1:T(8,128)(4,1)S(1)} %copy.73, bf16[256,1,4,128]{0,3,2,1:T(8,128)(2,1)S(1)} %get-tuple-element.869, ...), kind=kOutput, calls=%fused_computation.40.clone.1 | convolution fusion | flops 275775488 | bytes 7086084 | tf_op jit(solution)/shard_map/while/body/eval_jaxpr/qghd,kgd->ghqk/dot_general | solution.py:105
  171.4 3.9 %copy.45 = bf16[4,1024,256]{2,1,0:T(8,128)(2,1)} copy(bf16[4,1024,256]{1,2,0:T(8,128)(2,1)} %get-tuple-element.424) | data formatting | bytes 4194304 | tf_op jit(solution)/shard_map/convert_element_type | solution.py:155
  177.2 57.0 %reduce-scatter.2.cloned.1.call-done = bf16[256,256]{1,0:T(8,128)(2,1)} async-done(((bf16[4096,256]{1,0:T(8,128)(2,1)}), bf16[256,256]{1,0:T(8,128)(2,1)}) %reduce-scatter.2.cloned.1.call-update) | async-done | bytes 131088 | tf_op jit(solution)/shard_map/reduce_scatter | solution.py:154
  234.2 1.6 fusion.75
  (151 shorter events, 50.2 us)
Async XLA Ops:
  7.2 2.4 copy-start
  7.2 44.2 %all-gather.3.cloned.1.call-start = ((), (), s32[]{:S(2)}) async-start(), calls=%async_computation.1 | async-start | bytes 1114112 | tf_op jit(solution)/shard_map/all_gather | solution.py:75
  7.9 82.4 %all-gather.5.cloned.1.call-start = ((), (), s32[]{:S(2)}) async-start(), calls=%async_computation.2 | async-start | bytes 1114112 | tf_op jit(solution)/shard_map/all_gather | solution.py:76
  8.7 225.6 %reduce-scatter.2.cloned.1.call-start = ((), (), s32[]{:S(2)}) async-start(), calls=%async_computation.3 | async-start | bytes 2228224 | tf_op jit(solution)/shard_map/reduce_scatter | solution.py:154
Sparse Core Ops, SparseCore 0:
  9.8 41.4 all-gather.2
  53.2 37.0 all-gather.4
  175.5 58.6 reduce-scatter.1
where the time goes:
time: 243 us; the launch traced here: 242 us
  waiting for transfers between devices  136 us (56%)
  matrix products  48.5 us (20%)
  local copies, waits for them, and re-layouts  22.7 us (9%)
  other arithmetic  17.7 us (7%)
  between operations  13.9 us (6%)
  loops' own time  3.33 us (1%)
    reduce_scatter x1, waiting for transfers between devices, per_device(): lax.psum_scatter(key_terms.astype(jnp.bfloat16), 'seq', scatter_dimension...  57 us
    all_gather x1, waiting for transfers between devices, per_device(): value_piece = lax.all_gather(value_rows, 'seq', axis=0, tiled=True)  39 us
    all_gather x1, waiting for transfers between devices, per_device(): key_piece = lax.all_gather(key_rows, 'seq', axis=0, tiled=True)  38.7 us
    dot_general x8, matrix products, masked_scores(): jnp.einsum('qghd,kgd->ghqk', query_heads, key_block, preferred_element_ty...  13.6 us
    dot_general x4, matrix products, backward_block(): jnp.einsum('qghd,kgd->ghqk', grad_heads, value_block, preferred_element_t...  9.81 us
    dot_general x4, matrix products, forward_block(): jnp.einsum('ghqk,kgd->ghqd', softmax_terms.astype(jnp.bfloat16), value_bl...  9.75 us
    dot_general x4, matrix products, backward_block(): jnp.einsum('ghqk,qghd->kgd', softmax_terms.astype(jnp.bfloat16), grad_hea...  6.03 us
    dot_general x4, matrix products, backward_block(): jnp.einsum('ghqk,kgd->qghd', dscores, key_block, preferred_element_type=j...  6.02 us
  transfers between devices with their start and end apart: 3, of which 3 were waited for; matrix products, arithmetic and copies ran while one was open for 2% of the time, Pallas kernels for 0%

commit v1 on v0

--- a/solution.py
+++ b/solution.py
@@ -72,7 +72,9 @@
         jnp.zeros(stat_shape, jnp.float32),
         jnp.zeros(stat_shape + (HD,), jnp.float32),
     )
-    key_piece = lax.all_gather(key_rows, "seq", axis=0, tiled=True)
+    key_piece = jnp.concatenate(
+        lax.all_to_all(jnp.stack([key_rows] * lax.axis_size("seq")), "seq", 0, 0), axis=0
+    )
     value_piece = lax.all_gather(value_rows, "seq", axis=0, tiled=True)
     block_rows, number = sub_blocks(key_piece.shape[0], limit)
 

time: 243 us -> 215 us (0.88)
  waiting for transfers between devices: 136 us -> 108 us
  starting transfers between devices: 0.11 us -> 8.69 us
  other arithmetic: 17.7 us -> 12.5 us
  matrix products: 48.5 us -> 44.8 us
    all_gather x1, waiting for transfers between devices: 38.7 us -> 15.1 us  [per_device(): lax.all_gather(key_rows, 'seq', axis=0, tiled=True)]
    all_to_all x0 -> x1, starting transfers between devices: none -> 8.57 us  [per_device(): lax.all_to_all(jnp.stack([key_rows] * lax.axis_size('seq')), 'seq', 0, 0)]
    and x8, other arithmetic: 5.9 us -> 0.65 us  [tile_allowed(): jnp.take(jnp.take(tile_mask, query_tiles, axis=0), key_tiles, axis=1) == 1]
    all_gather x1, waiting for transfers between devices: 39 us -> 34.1 us  [per_device(): value_piece = lax.all_gather(value_rows, 'seq', axis=0, tiled=True)]
    dot_general x8, matrix products: 13.6 us -> 9.85 us  [masked_scores(): jnp.einsum('qghd,kgd->ghqk', query_heads, key_block, preferred_element_ty...]
  transfers between devices with their start and end apart: 3 -> 4, of which waited for: 3 -> 3; matrix products, arithmetic and copies ran while one was open for 2% -> 15% of each run, Pallas kernels for 0% -> 0%
where the time goes in v1:
time: 215 us
  waiting for transfers between devices  108 us (50%)
  matrix products  44.8 us (21%)
  local copies, waits for them, and re-layouts  23.8 us (11%)
  between operations  13.9 us (6%)
  other arithmetic  12.5 us (6%)
  starting transfers between devices  8.69 us (4%)
  loops' own time  3.31 us (2%)
    reduce_scatter x1, waiting for transfers between devices, per_device(): lax.psum_scatter(key_terms.astype(jnp.bfloat16), 'seq', scatter_dimension...  57 us
    all_gather x1, waiting for transfers between devices, per_device(): value_piece = lax.all_gather(value_rows, 'seq', axis=0, tiled=True)  34.1 us
    all_gather x1, waiting for transfers between devices, per_device(): lax.all_gather(key_rows, 'seq', axis=0, tiled=True)  15.1 us
    dot_general x8, matrix products, masked_scores(): jnp.einsum('qghd,kgd->ghqk', query_heads, key_block, preferred_element_ty...  9.85 us
    dot_general x4, matrix products, backward_block(): jnp.einsum('qghd,kgd->ghqk', grad_heads, value_block, preferred_element_t...  9.84 us
    dot_general x4, matrix products, forward_block(): jnp.einsum('ghqk,kgd->ghqd', softmax_terms.astype(jnp.bfloat16), value_bl...  9.74 us
    all_to_all x1, starting transfers between devices, per_device(): lax.all_to_all(jnp.stack([key_rows] * lax.axis_size('seq')), 'seq', 0, 0)  8.57 us
    dot_general x4, matrix products, backward_block(): jnp.einsum('ghqk,qghd->kgd', softmax_terms.astype(jnp.bfloat16), grad_hea...  6.15 us
  transfers between devices with their start and end apart: 4, of which 3 were waited for; matrix products, arithmetic and copies ran while one was open for 15% of the time, Pallas kernels for 0%

profile of v1, /device:TPU:2, one launch (start us, length us, event | category | flops | bytes accessed | tf_op | source)
XLA Modules:
  0.0 214.5 jit_solution(3538466680637001799)
XLA Ops:
  7.9 2.0 stack.2
  10.0 8.6 %all-to-all-start = ((bf16[16,256,128]{2,1,0:T(8,128)(2,1)}), bf16[16,256,128]{2,1,0:T(8,128)(2,1)S(1)}, u32[]{:S(2)}, u32[]{:S(2)}) async-start(bf16[16,256,128]{2,1,0:T(8,128)(2,1)} %stack.2), calls=%async_computation | async-start | bytes 2097152 | tf_op jit(solution)/shard_map/all_to_all | solution.py:76
  22.3 34.1 %all-gather.3.cloned.1.call-done = bf16[4096,128]{1,0:T(8,128)(2,1)} async-done(((bf16[256,128]{1,0:T(8,128)(2,1)}), bf16[4096,128]{1,0:T(8,128)(2,1)}) %all-gather.3.cloned.1.call-update) | async-done | bytes 1048592 | tf_op jit(solution)/shard_map/all_gather | solution.py:78
  56.4 24.5 %while.35 = (s32[]{:T(128)}, f32[1,4,256]{2,1,0:T(4,128)S(1)}, f32[1,4,256]{2,1,0:T(4,128)S(1)}, f32[1,4,256,128]{3,2,1,0:T(8,128)S(1)}, s32[32]{0:T(128)S(1)}, ...) while((s32[]{:T(128)}, f32[1,4,256]{2,1,0:T(4,128)S(1)}, ...), condition=%wide.region_3.6_spmd.clone, body=%wide.region_0.5_spmd.clone.sunk | while | flops 551443584 | bytes 16618426 | solution.py:90
  60.0 2.4 %fusion.103 = f32[1,4,256,128]{3,2,1,0:T(8,128)S(1)} fusion(f32[1024,256,4]{1,0,2:T(8,128)S(1)} %get-tuple-element.745, f32[4,256]{1,0:T(4,128)S(1)} %bitcast.247, pred[256,1024]{0,1:T(8,128)(4,1)S(1)} %copy.70, f32[1,4,256,128]{3,2,1,0:T(8,128)S(1)} %get-tuple-element.783, bf16[4096,128]{1,0:T(8,128)(2,1)} %get-tuple-element.807, ...), kind=kOutput, calls=%fused_computation.12.clone.1 | convolution fusion | flops 274071552 | bytes 5775365 | tf_op jit(solution)/shard_map/while/body/eval_jaxpr/ghqk,kgd->ghqd/dot_general | solution.py:61
  66.1 2.4 %fusion.103 = f32[1,4,256,128]{3,2,1,0:T(8,128)S(1)} fusion(f32[1024,256,4]{1,0,2:T(8,128)S(1)} %get-tuple-element.745, f32[4,256]{1,0:T(4,128)S(1)} %bitcast.247, pred[256,1024]{0,1:T(8,128)(4,1)S(1)} %copy.70, f32[1,4,256,128]{3,2,1,0:T(8,128)S(1)} %get-tuple-element.783, bf16[4096,128]{1,0:T(8,128)(2,1)} %get-tuple-element.807, ...), kind=kOutput, calls=%fused_computation.12.clone.1 | convolution fusion | flops 274071552 | bytes 5775365 | tf_op jit(solution)/shard_map/while/body/eval_jaxpr/ghqk,kgd->ghqd/dot_general | solution.py:61
  72.3 2.4 %fusion.103 = f32[1,4,256,128]{3,2,1,0:T(8,128)S(1)} fusion(f32[1024,256,4]{1,0,2:T(8,128)S(1)} %get-tuple-element.745, f32[4,256]{1,0:T(4,128)S(1)} %bitcast.247, pred[256,1024]{0,1:T(8,128)(4,1)S(1)} %copy.70, f32[1,4,256,128]{3,2,1,0:T(8,128)S(1)} %get-tuple-element.783, bf16[4096,128]{1,0:T(8,128)(2,1)} %get-tuple-element.807, ...), kind=kOutput, calls=%fused_computation.12.clone.1 | convolution fusion | flops 274071552 | bytes 5775365 | tf_op jit(solution)/shard_map/while/body/eval_jaxpr/ghqk,kgd->ghqd/dot_general | solution.py:61
  78.4 2.4 %fusion.103 = f32[1,4,256,128]{3,2,1,0:T(8,128)S(1)} fusion(f32[1024,256,4]{1,0,2:T(8,128)S(1)} %get-tuple-element.745, f32[4,256]{1,0:T(4,128)S(1)} %bitcast.247, pred[256,1024]{0,1:T(8,128)(4,1)S(1)} %copy.70, f32[1,4,256,128]{3,2,1,0:T(8,128)S(1)} %get-tuple-element.783, bf16[4096,128]{1,0:T(8,128)(2,1)} %get-tuple-element.807, ...), kind=kOutput, calls=%fused_computation.12.clone.1 | convolution fusion | flops 274071552 | bytes 5775365 | tf_op jit(solution)/shard_map/while/body/eval_jaxpr/ghqk,kgd->ghqd/dot_general | solution.py:61
  81.2 15.1 %all-gather.5.cloned.1.call-done = bf16[4096,128]{1,0:T(8,128)(2,1)} async-done(((bf16[256,128]{1,0:T(8,128)(2,1)}), bf16[4096,128]{1,0:T(8,128)(2,1)}) %all-gather.5.cloned.1.call-update) | async-done | bytes 1048592 | tf_op jit(solution)/shard_map/all_gather | solution.py:130
  96.3 47.3 %while.36 = (s32[]{:T(128)}, f32[256,1,4,128]{0,3,2,1:T(8,128)S(1)}, bf16[4,1024,256]{1,2,0:T(8,128)(2,1)}, s32[4]{0:T(128)S(1)}, bf16[4096,128]{1,0:T(8,128)(2,...) while((s32[]{:T(128)}, ...), condition=%wide.region_6.9_spmd.clone, body=%wide.region_5.8_spmd.clone.sunk | while | flops 1357005952 | bytes 25215972 | solution.py:147
  99.3 1.7 fusion.114
  100.9 1.5 fusion.117
  102.5 2.5 %fusion.115 = bf16[1,4,256,1024]{2,3,1,0:T(8,128)(2,1)S(1)} fusion(f32[1024,256,4]{1,0,2:T(8,128)S(1)} %fusion.114, f32[4,256]{1,0:T(4,128)S(1)} %bitcast.253, f32[4,256]{1,0:T(4,128)S(1)} %bitcast.255, pred[256,1024]{0,1:T(8,128)(4,1)S(1)} %copy.73, bf16[256,1,4,128]{0,3,2,1:T(8,128)(2,1)S(1)} %get-tuple-element.869, ...), kind=kOutput, calls=%fused_computation.40.clone.1 | convolution fusion | flops 275775488 | bytes 7086084 | tf_op jit(solution)/shard_map/while/body/eval_jaxpr/qghd,kgd->ghqk/dot_general | solution.py:107
  111.1 1.6 fusion.114
  112.8 1.5 fusion.117
  114.3 2.5 %fusion.115 = bf16[1,4,256,1024]{2,3,1,0:T(8,128)(2,1)S(1)} fusion(f32[1024,256,4]{1,0,2:T(8,128)S(1)} %fusion.114, f32[4,256]{1,0:T(4,128)S(1)} %bitcast.253, f32[4,256]{1,0:T(4,128)S(1)} %bitcast.255, pred[256,1024]{0,1:T(8,128)(4,1)S(1)} %copy.73, bf16[256,1,4,128]{0,3,2,1:T(8,128)(2,1)S(1)} %get-tuple-element.869, ...), kind=kOutput, calls=%fused_computation.40.clone.1 | convolution fusion | flops 275775488 | bytes 7086084 | tf_op jit(solution)/shard_map/while/body/eval_jaxpr/qghd,kgd->ghqk/dot_general | solution.py:107
  122.9 1.6 fusion.114
  124.6 1.5 fusion.117
  126.1 2.5 %fusion.115 = bf16[1,4,256,1024]{2,3,1,0:T(8,128)(2,1)S(1)} fusion(f32[1024,256,4]{1,0,2:T(8,128)S(1)} %fusion.114, f32[4,256]{1,0:T(4,128)S(1)} %bitcast.253, f32[4,256]{1,0:T(4,128)S(1)} %bitcast.255, pred[256,1024]{0,1:T(8,128)(4,1)S(1)} %copy.73, bf16[256,1,4,128]{0,3,2,1:T(8,128)(2,1)S(1)} %get-tuple-element.869, ...), kind=kOutput, calls=%fused_computation.40.clone.1 | convolution fusion | flops 275775488 | bytes 7086084 | tf_op jit(solution)/shard_map/while/body/eval_jaxpr/qghd,kgd->ghqk/dot_general | solution.py:107
  134.8 1.7 fusion.114
  138.0 2.5 %fusion.115 = bf16[1,4,256,1024]{2,3,1,0:T(8,128)(2,1)S(1)} fusion(f32[1024,256,4]{1,0,2:T(8,128)S(1)} %fusion.114, f32[4,256]{1,0:T(4,128)S(1)} %bitcast.253, f32[4,256]{1,0:T(4,128)S(1)} %bitcast.255, pred[256,1024]{0,1:T(8,128)(4,1)S(1)} %copy.73, bf16[256,1,4,128]{0,3,2,1:T(8,128)(2,1)S(1)} %get-tuple-element.869, ...), kind=kOutput, calls=%fused_computation.40.clone.1 | convolution fusion | flops 275775488 | bytes 7086084 | tf_op jit(solution)/shard_map/while/body/eval_jaxpr/qghd,kgd->ghqk/dot_general | solution.py:107
  143.6 3.9 %copy.45 = bf16[4,1024,256]{2,1,0:T(8,128)(2,1)} copy(bf16[4,1024,256]{1,2,0:T(8,128)(2,1)} %get-tuple-element.424) | data formatting | bytes 4194304 | tf_op jit(solution)/shard_map/convert_element_type | solution.py:157
  149.4 57.0 %reduce-scatter.2.cloned.1.call-done = bf16[256,256]{1,0:T(8,128)(2,1)} async-done(((bf16[4096,256]{1,0:T(8,128)(2,1)}), bf16[256,256]{1,0:T(8,128)(2,1)}) %reduce-scatter.2.cloned.1.call-update) | async-done | bytes 131088 | tf_op jit(solution)/shard_map/reduce_scatter | solution.py:156
  206.4 1.6 fusion.75
  (158 shorter events, 44.3 us)
Async XLA Ops:
  7.2 13.0 %copy-start = (s32[32,32]{1,0:T(8,128)S(1)}, s32[32,32]{1,0:T(8,128)}, u32[]{:S(2)}) copy-start(s32[32,32]{1,0:T(8,128)} %param.19) | copy-start | bytes 12292
  7.2 49.2 %copy-start.2 = (s32[32]{0:T(128)S(1)}, s32[32]{0:T(128)}, u32[]{:S(2)}) copy-start(s32[32]{0:T(128)} %param.18) | copy-start | bytes 388
  7.2 14.9 %copy-start.1 = (bf16[256,512]{1,0:T(8,128)(2,1)S(1)}, bf16[256,512]{1,0:T(8,128)(2,1)}, u32[]{:S(2)}) copy-start(bf16[256,512]{1,0:T(8,128)(2,1)} %param.17) | copy-start | bytes 786436
  7.2 49.2 %all-gather.3.cloned.1.call-start = ((), (), s32[]{:S(2)}) async-start(), calls=%async_computation.2 | async-start | bytes 1114112 | tf_op jit(solution)/shard_map/all_gather | solution.py:78
  10.0 46.4 %all-to-all-start = ((bf16[16,256,128]{2,1,0:T(8,128)(2,1)}), bf16[16,256,128]{2,1,0:T(8,128)(2,1)S(1)}, u32[]{:S(2)}, u32[]{:S(2)}) async-start(bf16[16,256,128]{2,1,0:T(8,128)(2,1)} %stack.2), calls=%async_computation | async-start | bytes 2097152 | tf_op jit(solution)/shard_map/all_to_all | solution.py:76
  18.5 77.7 %all-gather.5.cloned.1.call-start = ((), (), s32[]{:S(2)}) async-start(), calls=%async_computation.3 | async-start | bytes 1114112 | tf_op jit(solution)/shard_map/all_gather | solution.py:130
  19.3 187.1 %reduce-scatter.2.cloned.1.call-start = ((), (), s32[]{:S(2)}) async-start(), calls=%async_computation.4 | async-start | bytes 2228224 | tf_op jit(solution)/shard_map/reduce_scatter | solution.py:156
Sparse Core Ops, SparseCore 0:
  9.8 46.4 all-gather.2
  58.2 38.0 all-gather.4
  147.7 58.6 reduce-scatter.1
